TPU v7x, 32 devices: a whole 2x2x4 slice. The times are simulated.
32 devices in a mesh: dp: 8 (over y, x, core), mp: 4 (over z).
Axes of the slice: x: 2, y: 2, z: 4, core: 2. Of those that a mesh axis runs over, the one named last changes fastest.
Arguments:
- tokens: bfloat16 [32, 512, 768], P('dp'), may hold values from -6 to 6
- doc_lengths: int32 [32, 4], P('dp'), may hold values from 1 to 256, 512 in all within a row
- w_query: bfloat16 [768, 768], P(None, 'mp'), may hold values from -0.21875 to 0.21875
- b_query: bfloat16 [768], P('mp'), may hold values from -3 to 3
- w_key: bfloat16 [768, 768], P(None, 'mp'), may hold values from -0.21875 to 0.21875
- w_value: bfloat16 [768, 768], P(None, 'mp'), may hold values from -0.21875 to 0.21875
- b_value: bfloat16 [768], P('mp'), may hold values from -3 to 3
- w_output: bfloat16 [768, 768], P('mp'), may hold values from -0.875 to 0.875
- b_output: bfloat16 [768], replicated, may hold values from -3 to 3
- gain_attn: bfloat16 [768], replicated, may hold values from 0.5 to 1.5
- shift_attn: bfloat16 [768], replicated, may hold values from -2 to 2
- w_expand: bfloat16 [768, 3072], P(None, 'mp'), may hold values from -0.21875 to 0.21875
- b_expand: bfloat16 [3072], P('mp'), may hold values from -3 to 3
- w_reduce: bfloat16 [3072, 768], P('mp'), may hold values from -0.21875 to 0.21875
- b_reduce: bfloat16 [768], replicated, may hold values from -2 to 2
- gain_ffn: bfloat16 [768], replicated, may hold values from 0.5 to 1.5
- shift_ffn: bfloat16 [768], replicated, may hold values from -2 to 2
- cotangent: bfloat16 [32, 512, 768], P('dp'), may hold values from -6 to 6
Outputs:
- output: bfloat16 [32, 512, 768], P('dp')
- grad_tokens: bfloat16 [32, 512, 768], P('dp')
- grad_w_query: float32 [768, 768], P(None, 'mp')
- grad_b_query: float32 [768], P('mp')
- grad_w_key: float32 [768, 768], P(None, 'mp')
- grad_w_value: float32 [768, 768], P(None, 'mp')
- grad_b_value: float32 [768], P('mp')
- grad_w_output: float32 [768, 768], P('mp')
- grad_b_output: float32 [768], replicated
- grad_gain_attn: float32 [768], replicated
- grad_shift_attn: float32 [768], replicated
- grad_w_expand: float32 [768, 3072], P(None, 'mp')
- grad_b_expand: float32 [3072], P('mp')
- grad_w_reduce: float32 [3072, 768], P('mp')
- grad_b_reduce: float32 [768], replicated
- grad_gain_ffn: float32 [768], replicated
- grad_shift_ffn: float32 [768], replicated
Inputs may be any that keep to these rules, and one draw needn't show every extreme that they name: `doc_lengths`: the 4 lengths of a row sum to 512, and the largest of every row is 256.
All inputs are finite; a program needn't handle non-finite values.
Results may differ from a plain program's by a relative error of at most 0.014.
Values sent between devices are 32-bit elements; how exact they have to be, the bound alone decides.
No kernel may reach another device: no remote copies, remote signals or barrier semaphores. Data moves between devices by JAX's collectives and lax.ppermute only.
A program may use at most 128 MiB of HBM per device.

v0:
```python
import jax
import jax.numpy as jnp
from jax import lax
from jax.sharding import PartitionSpec as P

HD = 64
norm_eps = 1e-12
masked_score = -1000000000.0


def layer_norm(hidden, gain_vec, shift_vec):
    center = hidden - jnp.mean(hidden, axis=-1, keepdims=True)
    spread = jnp.mean(center * center, axis=-1, keepdims=True)
    return center * lax.rsqrt(spread + norm_eps) * gain_vec + shift_vec


def gelu_tanh(values):
    return jax.nn.gelu(values, approximate=True)


def segment_ids(doc_lengths, length):
    doc_ends = jnp.cumsum(doc_lengths, axis=-1)
    position = jnp.arange(length, dtype=jnp.int32)
    return jnp.sum((position[None, :, None] >= doc_ends[:, None, :]).astype(jnp.int32), axis=-1)


def masked_scores(queries, keys_row, segment):
    scores = jnp.einsum(
        "qhd,khd->hqk", queries, keys_row, preferred_element_type=jnp.float32
    ) * HD ** (-0.5)
    same_doc = segment[:, None] == segment[None, :]
    return jnp.where(same_doc[None], scores, masked_score)


def attend_forward(packed):
    queries, keys_row, values_row, segment = packed
    scores = masked_scores(queries, keys_row, segment)
    highest = jnp.max(scores, axis=-1, keepdims=True)
    exponent = jnp.exp(scores - highest)
    totals = jnp.sum(exponent, axis=-1, keepdims=True)
    attn_probs = exponent / totals
    log_total = highest[..., 0] + jnp.log(totals[..., 0])
    context = jnp.einsum(
        "hqk,khd->qhd",
        attn_probs.astype(jnp.bfloat16),
        values_row,
        preferred_element_type=jnp.float32,
    )
    return (context.astype(jnp.bfloat16), log_total, attn_probs)


def recomputed_probs(packed):
    queries, keys_row, values_row, segment, log_total, grad_context = packed
    return jnp.exp(masked_scores(queries, keys_row, segment) - log_total[..., None])


def attend_backward(packed, attn_probs):
    queries, keys_row, values_row, segment, log_total, grad_context = packed
    grad_probs = jnp.einsum(
        "qhd,khd->hqk", grad_context, values_row, preferred_element_type=jnp.float32
    )
    inner_sum = jnp.sum(attn_probs * grad_probs, axis=-1, keepdims=True)
    grad_scores = (attn_probs * (grad_probs - inner_sum)).astype(jnp.bfloat16)
    grad_query = jnp.einsum(
        "hqk,khd->qhd", grad_scores, keys_row, preferred_element_type=jnp.float32
    ) * HD ** (-0.5)
    grad_key = jnp.einsum(
        "hqk,qhd->khd", grad_scores, queries, preferred_element_type=jnp.float32
    ) * HD ** (-0.5)
    grad_value = jnp.einsum(
        "hqk,qhd->khd",
        attn_probs.astype(jnp.bfloat16),
        grad_context,
        preferred_element_type=jnp.float32,
    )
    return (
        grad_query.astype(jnp.bfloat16),
        grad_key.astype(jnp.bfloat16),
        grad_value.astype(jnp.bfloat16),
    )


def local(
    tokens,
    doc_lengths,
    w_query,
    b_query,
    w_key,
    w_value,
    b_value,
    w_output,
    b_output,
    gain_attn,
    shift_attn,
    w_expand,
    b_expand,
    w_reduce,
    b_reduce,
    gain_ffn,
    shift_ffn,
    cotangent,
):
    row_count, length, model_width = tokens.shape
    heads_local = w_query.shape[1] // HD
    token_count = row_count * length
    inputs = tokens.reshape(token_count, model_width)
    segment = segment_ids(doc_lengths, length)
    queries = (
        jnp.dot(inputs, w_query, preferred_element_type=jnp.float32) + b_query.astype(jnp.float32)
    ).astype(jnp.bfloat16)
    keys_all = jnp.dot(inputs, w_key, preferred_element_type=jnp.float32).astype(jnp.bfloat16)
    values_all = (
        jnp.dot(inputs, w_value, preferred_element_type=jnp.float32) + b_value.astype(jnp.float32)
    ).astype(jnp.bfloat16)
    head_split = (row_count, length, heads_local, HD)
    packed = (
        queries.reshape(head_split),
        keys_all.reshape(head_split),
        values_all.reshape(head_split),
        segment,
    )
    context, log_total = lax.map(lambda row_item: attend_forward(row_item)[:2], packed)
    context = context.reshape(token_count, heads_local * HD)
    attended = lax.psum(
        jnp.dot(context, w_output, preferred_element_type=jnp.float32), "mp"
    ) + b_output.astype(jnp.float32)
    residual_one = inputs.astype(jnp.float32) + attended
    normed, attn_norm_back = jax.vjp(
        layer_norm, residual_one, gain_attn.astype(jnp.float32), shift_attn.astype(jnp.float32)
    )
    normed_low = normed.astype(jnp.bfloat16)
    hidden = jnp.dot(normed_low, w_expand, preferred_element_type=jnp.float32) + b_expand.astype(
        jnp.float32
    )
    gelu_value, gelu_back = jax.vjp(gelu_tanh, hidden)
    active = gelu_value.astype(jnp.bfloat16)
    mixed_out = lax.psum(
        jnp.dot(active, w_reduce, preferred_element_type=jnp.float32), "mp"
    ) + b_reduce.astype(jnp.float32)
    residual_two = normed + mixed_out
    output, ffn_norm_back = jax.vjp(
        layer_norm, residual_two, gain_ffn.astype(jnp.float32), shift_ffn.astype(jnp.float32)
    )
    grad_output = cotangent.reshape(token_count, model_width).astype(jnp.float32)
    grad_two, grad_gain_ffn, grad_shift_ffn = ffn_norm_back(grad_output)
    grad_two_low = grad_two.astype(jnp.bfloat16)
    grad_b_reduce = jnp.sum(grad_two, axis=0)
    grad_w_reduce = jnp.einsum(
        "tf,td->fd", active, grad_two_low, preferred_element_type=jnp.float32
    )
    grad_active = jnp.einsum(
        "td,fd->tf", grad_two_low, w_reduce, preferred_element_type=jnp.float32
    )
    grad_hidden = gelu_back(grad_active)[0].astype(jnp.bfloat16)
    grad_b_expand = jnp.sum(grad_hidden.astype(jnp.float32), axis=0)
    grad_w_expand = jnp.einsum(
        "td,tf->df", normed_low, grad_hidden, preferred_element_type=jnp.float32
    )
    grad_normed = grad_two + lax.psum(
        jnp.einsum("tf,df->td", grad_hidden, w_expand, preferred_element_type=jnp.float32), "mp"
    )
    grad_one, grad_gain_attn, grad_shift_attn = attn_norm_back(grad_normed)
    grad_b_output = jnp.sum(grad_one, axis=0)
    grad_one_low = grad_one.astype(jnp.bfloat16)
    grad_w_output = jnp.einsum(
        "tc,td->cd", context, grad_one_low, preferred_element_type=jnp.float32
    )
    grad_context = jnp.einsum(
        "td,cd->tc", grad_one_low, w_output, preferred_element_type=jnp.float32
    ).astype(jnp.bfloat16)
    packed_back = packed + (log_total, grad_context.reshape(head_split))
    grad_query, grad_key, grad_value = lax.map(
        lambda row_item: attend_backward(row_item, recomputed_probs(row_item)), packed_back
    )
    grad_query = grad_query.reshape(token_count, heads_local * HD)
    grad_key = grad_key.reshape(token_count, heads_local * HD)
    grad_value = grad_value.reshape(token_count, heads_local * HD)
    grad_b_query = jnp.sum(grad_query.astype(jnp.float32), axis=0)
    grad_b_value = jnp.sum(grad_value.astype(jnp.float32), axis=0)
    grad_w_query = jnp.einsum("td,tc->dc", inputs, grad_query, preferred_element_type=jnp.float32)
    grad_w_key = jnp.einsum("td,tc->dc", inputs, grad_key, preferred_element_type=jnp.float32)
    grad_w_value = jnp.einsum("td,tc->dc", inputs, grad_value, preferred_element_type=jnp.float32)
    back_terms = jnp.einsum("tc,dc->td", grad_query, w_query, preferred_element_type=jnp.float32)
    back_terms = back_terms + jnp.einsum(
        "tc,dc->td", grad_key, w_key, preferred_element_type=jnp.float32
    )
    back_terms = back_terms + jnp.einsum(
        "tc,dc->td", grad_value, w_value, preferred_element_type=jnp.float32
    )
    grad_inputs = grad_one + lax.psum(back_terms, "mp")
    summed = lax.psum(
        (
            grad_w_query,
            grad_b_query,
            grad_w_key,
            grad_w_value,
            grad_b_value,
            grad_w_output,
            grad_b_output,
            grad_gain_attn,
            grad_shift_attn,
            grad_w_expand,
            grad_b_expand,
            grad_w_reduce,
            grad_b_reduce,
            grad_gain_ffn,
            grad_shift_ffn,
        ),
        "dp",
    )
    (
        grad_w_query,
        grad_b_query,
        grad_w_key,
        grad_w_value,
        grad_b_value,
        grad_w_output,
        grad_b_output,
        grad_gain_attn,
        grad_shift_attn,
    ) = summed[:9]
    grad_w_expand, grad_b_expand, grad_w_reduce, grad_b_reduce, grad_gain_ffn, grad_shift_ffn = (
        summed[9:]
    )
    return (
        output.astype(jnp.bfloat16).reshape(row_count, length, model_width),
        grad_inputs.astype(jnp.bfloat16).reshape(row_count, length, model_width),
        grad_w_query,
        grad_b_query,
        grad_w_key,
        grad_w_value,
        grad_b_value,
        grad_w_output,
        grad_b_output,
        grad_gain_attn,
        grad_shift_attn,
        grad_w_expand,
        grad_b_expand,
        grad_w_reduce,
        grad_b_reduce,
        grad_gain_ffn,
        grad_shift_ffn,
    )


def solution(mesh):
    placed = (
        P("dp", None, None),
        P("dp", None),
        P(None, "mp"),
        P("mp"),
        P(None, "mp"),
        P(None, "mp"),
        P("mp"),
        P("mp", None),
        P(),
        P(),
        P(),
        P(None, "mp"),
        P("mp"),
        P("mp", None),
        P(),
        P(),
        P(),
        P("dp", None, None),
    )
    return jax.shard_map(
        local,
        mesh=mesh,
        in_specs=placed,
        out_specs=(
            P("dp", None, None),
            P("dp", None, None),
            P(None, "mp"),
            P("mp"),
            P(None, "mp"),
            P(None, "mp"),
            P("mp"),
            P("mp", None),
            P(),
            P(),
            P(),
            P(None, "mp"),
            P("mp"),
            P("mp", None),
            P(),
            P(),
            P(),
        ),
        check_vma=False,
    )
```

profile of v0, /device:TPU:0, one launch (start us, length us, event | category | flops | bytes accessed | tf_op | source)
XLA Modules:
  0.0 1190.3 jit_solution(14834933972039977539)
XLA Ops:
  9.6 3.1 fusion.66
  13.4 3.1 fusion.67
  17.3 3.1 convolution_convert_fusion.1
  24.0 16.3 %while.26 = (s32[]{:T(128)}, bf16[4,512,3,64]{1,3,2,0:T(8,128)(2,1)}, f32[4,3,512]{2,1,0:T(4,128)}, bf16[4,512,3,64]{1,3,2,0:T(8,128)(2,1)S(1)}, s32[4,512]{1,0:...) while((s32[]{:T(128)}, ...), condition=%wide.region_5.6_spmd, body=%wide.region_2.5_spmd.sunk | while | flops 211122688 | bytes 11335781 | solution.py:122
  25.7 1.8 fusion.136
  29.8 1.8 fusion.136
  33.9 1.8 fusion.136
  38.0 1.8 fusion.136
  40.4 2.0 copy.68
  42.6 4.7 fusion.77
  51.0 222.0 %all-reduce.8.cloned.1.call-done = f32[2048,768]{1,0:T(8,128)} async-done(((f32[2048,768]{1,0:T(8,128)}), f32[2048,768]{1,0:T(8,128)}) %all-reduce.8.cloned.1.call-update) | async-done | bytes 6291472 | tf_op jit(solution)/shard_map/psum | solution.py:124
  273.0 4.6 fusion.76
  280.3 5.3 multiply_convert_fusion.1
  285.7 1.8 copy-done.37
  287.4 4.5 fusion.78
  295.8 218.1 %all-reduce.10.cloned.1.call-done = f32[2048,768]{1,0:T(8,128)} async-done(((f32[2048,768]{1,0:T(8,128)}), f32[2048,768]{1,0:T(8,128)}) %all-reduce.10.cloned.1.call-update) | async-done | bytes 6291472 | tf_op jit(solution)/shard_map/psum | solution.py:137
  513.9 5.7 fusion.75
  521.5 3.0 fusion.64
  524.6 4.3 fusion.74
  528.9 7.5 convert_reduce_fusion.1
  536.4 1.7 copy-done.36
  538.2 4.5 fusion.79
  542.9 221.7 %all-reduce.12.cloned.1.call-done = f32[2048,768]{1,0:T(8,128)} async-done(((f32[2048,768]{1,0:T(8,128)}), f32[2048,768]{1,0:T(8,128)}) %all-reduce.12.cloned.1.call-update) | async-done | bytes 6291472 | tf_op jit(solution)/shard_map/psum | solution.py:159
  764.6 8.1 multiply_reduce_fusion.1
  772.8 4.3 fusion.73
  777.1 2.6 copy-done.3
  786.7 35.2 %while.27 = (s32[]{:T(128)}, bf16[4,512,3,64]{1,3,2,0:T(8,128)(2,1)}, bf16[4,512,3,64]{1,3,2,0:T(8,128)(2,1)}, bf16[4,512,3,64]{1,3,2,0:T(8,128)(2,1)}, bf16[4,5...) while((s32[]{:T(128)}, ...), condition=%wide.region_19.20_spmd, body=%wide.region_17.19_spmd.sunk | while | flops 511146496 | bytes 26127484 | solution.py:172
  788.3 1.5 fusion.145
  805.9 1.5 fusion.145
  814.7 1.5 fusion.145
  821.9 1.8 copy.74
  823.9 1.7 copy.73
  828.8 3.7 add_add_fusion.2
  832.8 7.1 fusion.82
  839.9 7.2 fusion.70
  847.1 1.7 convolution_bitcast_fusion
  848.8 1.7 convolution_bitcast_fusion.2
  850.5 1.7 convolution_bitcast_fusion.1
  852.1 1.9 fusion.72
  854.0 2.5 convert_reduce_fusion
  857.0 197.5 %all-reduce.14.cloned.1.call-done = f32[2048,768]{1,0:T(8,128)} async-done(((f32[2048,768]{1,0:T(8,128)}), f32[2048,768]{1,0:T(8,128)}) %all-reduce.14.cloned.1.call-update) | async-done | bytes 6291472 | tf_op jit(solution)/shard_map/psum | solution.py:190
  1054.5 6.8 add_reduce_fusion
  1061.3 26.0 %all-reduce = (f32[192]{0:T(256)}, f32[192]{0:T(256)}, f32[768]{0:T(1024)}, f32[768]{0:T(1024)}, f32[768]{0:T(1024)}, /*index=5*/f32[768]{0:T(1024)}, f32[768]{0:T(1024)}, f32[768]{0:T(1024)}, f32[768]{0:T(1024)}) all-reduce(f32[192]{0:T(256)S(1)} %reduce_sum.226, f32[192]{0:T(256)S(1)} %reduce_sum.228, ...), channel_id=1, replica_groups=mesh['dp'=8,'mp'=4] {'dp'}, use_global_device_ids=true, to_apply=%region_23.24 | all-reduce | flops 5760 | bytes 46080 | tf_op jit(solution)/shard_map/psum | solution.py:191
  1087.4 85.5 %all-reduce.16.cloned.1.call-done = (f32[768,192]{0,1:T(8,128)}, f32[768,192]{0,1:T(8,128)}, f32[768,192]{0,1:T(8,128)}, f32[192,768]{1,0:T(8,128)}, f32[768,768]{1,0:T(8,128)}, /*index=5*/f32[768,768]{1,0:T(8,128)}) async-done(((f32[768,192]{0,1:T(8,128)}, f32[768,192]{0,1:T(8,128)}, f32[768,192]{0,1:T(8,128)}, f32[192,768]{1,0:T(8,128)}, f32[768,768]{1,0:T(8,128)}, /*index=5*/f32[768,768]{1,0:T(8,128)}), ...) | async-done | bytes 7077904 | tf_op jit(solution)/shard_map/psum | solution.py:191
  1172.8 2.1 copy.122
  1174.9 2.0 copy.123
  1176.9 1.9 copy.124
  1178.8 1.9 copy.125
  (196 shorter events, 73.5 us)
Async XLA Ops:
  7.2 273.1 %copy-start = (bf16[768,768]{1,0:T(8,128)(2,1)S(1)}, bf16[768,768]{1,0:T(8,128)(2,1)}, u32[]{:S(2)}) copy-start(bf16[768,768]{1,0:T(8,128)(2,1)} %param.33) | copy-start | bytes 3538948
  7.2 265.8 %all-reduce.8.cloned.1.call-start = ((), (), s32[]{:S(2)}) async-start(), calls=%async_computation | async-start | bytes 12582912 | tf_op jit(solution)/shard_map/psum | solution.py:124
  40.4 2.0 copy-start.10
  40.4 6.9 copy-start.20
  42.6 5.2 copy-start.32
  42.6 5.8 copy-start.33
  47.3 466.5 %all-reduce.10.cloned.1.call-start = ((), (), s32[]{:S(2)}) async-start(), calls=%async_computation.1 | async-start | bytes 12582912 | tf_op jit(solution)/shard_map/psum | solution.py:137
  277.6 2.7 copy-start.2
  277.6 0.9 copy-start.18
  277.6 0.9 copy-start.24
  278.5 7.1 copy-start.21
  278.5 1.8 copy-start.30
  280.3 5.4 copy-start.11
  280.3 7.1 copy-start.34
  285.6 1.8 copy-start.37
  291.9 472.7 %all-reduce.12.cloned.1.call-start = ((), (), s32[]{:S(2)}) async-start(), calls=%async_computation.2 | async-start | bytes 12582912 | tf_op jit(solution)/shard_map/psum | solution.py:159
  519.6 1.9 copy-start.5
  519.6 1.9 copy-start.23
  520.4 4.1 copy-start.28
  521.5 7.4 slice-start.2
  524.5 4.4 copy-start.31
  524.5 4.4 copy-start.35
  524.6 4.4 slice-start.3
  528.9 7.5 copy-start.6
  528.9 7.5 copy-start.25
  536.4 1.8 copy-start.36
  542.7 222.0 %copy-start.19 = (f32[768]{0:T(1024)S(1)}, f32[768]{0:T(1024)}, u32[]{:S(2)}) copy-start(f32[768]{0:T(1024)} %convert_element_type.127) | copy-start | bytes 9220
  542.7 222.0 %copy-start.26 = (f32[2048]{0:T(1024)S(1)}, f32[2048]{0:T(1024)}, u32[]{:S(2)}) copy-start(f32[2048]{0:T(1024)} %copy-done.25) | copy-start | bytes 24580
  542.7 230.1 %copy-start.22 = (f32[2048]{0:T(1024)S(1)}, f32[2048]{0:T(1024)}, u32[]{:S(2)}) copy-start(f32[2048]{0:T(1024)} %copy-done.21) | copy-start | bytes 24580
  542.7 511.8 %all-reduce.14.cloned.1.call-start = ((), (), s32[]{:S(2)}) async-start(), calls=%async_computation.3 | async-start | bytes 12582912 | tf_op jit(solution)/shard_map/psum | solution.py:190
  772.8 6.9 copy-start.14
  777.1 2.7 copy-start.3
  821.9 4.0 copy-start.7
  821.9 4.8 copy-start.15
  826.5 1.3 copy-start.16
  827.7 1.1 copy-start.17
  832.6 340.3 %all-reduce.16.cloned.1.call-start = ((), (), s32[]{:S(2)}) async-start(), calls=%async_computation.4 | async-start | bytes 14155776 | tf_op jit(solution)/shard_map/psum | solution.py:191
  832.8 7.1 copy-start.38
  839.9 7.2 copy-start.4
  847.1 5.0 slice-start
  848.8 3.3 slice-start.1
  854.0 2.6 copy-start.8
  854.0 2.6 copy-start.9
  857.0 204.3 %copy-start.27 = (f32[768]{0:T(1024)S(1)}, f32[768]{0:T(1024)}, u32[]{:S(2)}) copy-start(f32[768]{0:T(1024)} %get-tuple-element.167) | copy-start | bytes 9220
  857.0 204.3 %copy-start.29 = (f32[768]{0:T(1024)S(1)}, f32[768]{0:T(1024)}, u32[]{:S(2)}) copy-start(f32[768]{0:T(1024)} %get-tuple-element.238) | copy-start | bytes 9220
  1172.8 7.9 copy-start.13
  1172.8 9.3 copy-start.12
  1172.8 10.7 copy-start.1
Sparse Core Ops, SparseCore 0:
  47.4 225.5 all-reduce.7
  292.0 221.7 all-reduce.9
  542.8 221.7 all-reduce.11
  832.7 221.7 all-reduce.13
  1059.6 113.1 all-reduce.15
where the time goes:
time: 1200 us; the launch traced here: 1190 us
  waiting for transfers between devices  945 us (79%)
  matrix products  99.4 us (8%)
  other arithmetic  62.1 us (5%)
  local copies, waits for them, and re-layouts  42 us (4%)
  blocking collectives  26 us (2%)
  between operations  14.6 us (1%)
    psum x1, waiting for transfers between devices, local(): lax.psum(jnp.dot(context, w_output, preferred_element_type=jnp.float32),...  222 us
    psum x1, waiting for transfers between devices, local(): lax.psum(jnp.einsum('tf,df->td', grad_hidden, w_expand, preferred_element...  222 us
    psum x1, waiting for transfers between devices, local(): lax.psum(jnp.dot(active, w_reduce, preferred_element_type=jnp.float32), '...  218 us
    psum x1, waiting for transfers between devices, local(): grad_inputs = grad_one + lax.psum(back_terms, 'mp')  198 us
    psum x1, waiting for transfers between devices, local(): lax.psum((grad_w_query, grad_b_query, grad_w_key, grad_w_value, grad_b_va...  85.5 us
    psum x1, blocking collectives, local(): lax.psum((grad_w_query, grad_b_query, grad_w_key, grad_w_value, grad_b_va...  26 us
  transfers between devices with their start and end apart: 5, of which 5 were waited for; matrix products, arithmetic and copies ran while one was open for 3% of the time, Pallas kernels for 0%

commit v1 on v0

--- a/solution.py
+++ b/solution.py
@@ -156,8 +156,11 @@
     grad_w_expand = jnp.einsum(
         "td,tf->df", normed_low, grad_hidden, preferred_element_type=jnp.float32
     )
-    grad_normed = grad_two + lax.psum(
-        jnp.einsum("tf,df->td", grad_hidden, w_expand, preferred_element_type=jnp.float32), "mp"
+    grad_normed = grad_two + jnp.sum(
+        lax.all_gather(
+            jnp.einsum("tf,df->td", grad_hidden, w_expand, preferred_element_type=jnp.float32), "mp"
+        ),
+        axis=0,
     )
     grad_one, grad_gain_attn, grad_shift_attn = attn_norm_back(grad_normed)
     grad_b_output = jnp.sum(grad_one, axis=0)

time: 1200 us -> 1400 us (1.17)
  waiting for transfers between devices: 945 us -> 1150 us
    all_gather x0 -> x1, waiting for transfers between devices: none -> 424 us  [local(): lax.all_gather(jnp.einsum('tf,df->td', grad_hidden, w_expand, preferred_e...]
    psum x1 -> x0, waiting for transfers between devices: 222 us -> none  [local(): lax.psum(jnp.einsum('tf,df->td', grad_hidden, w_expand, preferred_element...]
  transfers between devices with their start and end apart: 5 -> 5, of which waited for: 5 -> 5; matrix products, arithmetic and copies ran while one was open for 3% -> 2% of each run, Pallas kernels for 0% -> 0%
where the time goes in v1:
time: 1400 us
  waiting for transfers between devices  1150 us (82%)
  matrix products  96.8 us (7%)
  other arithmetic  69.1 us (5%)
  local copies, waits for them, and re-layouts  38 us (3%)
  blocking collectives  26 us (2%)
  between operations  14.5 us (1%)
    all_gather x1, waiting for transfers between devices, local(): lax.all_gather(jnp.einsum('tf,df->td', grad_hidden, w_expand, preferred_e...  424 us
    psum x1, waiting for transfers between devices, local(): lax.psum(jnp.dot(context, w_output, preferred_element_type=jnp.float32),...  224 us
    psum x1, waiting for transfers between devices, local(): lax.psum(jnp.dot(active, w_reduce, preferred_element_type=jnp.float32), '...  221 us
    psum x1, waiting for transfers between devices, local(): grad_inputs = grad_one + lax.psum(back_terms, 'mp')  197 us
    psum x1, waiting for transfers between devices, local(): lax.psum((grad_w_query, grad_b_query, grad_w_key, grad_w_value, grad_b_va...  85.5 us
  transfers between devices with their start and end apart: 5, of which 5 were waited for; matrix products, arithmetic and copies ran while one was open for 2% of the time, Pallas kernels for 0%

profile of v1, /device:TPU:0, one launch (start us, length us, event | category | flops | bytes accessed | tf_op | source)
XLA Modules:
  0.0 1397.1 jit_solution(16497363538630895069)
XLA Ops:
  9.6 3.1 fusion.66
  13.4 3.1 fusion.67
  17.3 3.1 convolution_convert_fusion.1
  24.0 16.3 %while.26 = (s32[]{:T(128)}, bf16[4,512,3,64]{1,3,2,0:T(8,128)(2,1)}, f32[4,3,512]{2,1,0:T(4,128)}, bf16[4,512,3,64]{1,3,2,0:T(8,128)(2,1)S(1)}, s32[4,512]{1,0:...) while((s32[]{:T(128)}, ...), condition=%wide.region_5.6_spmd, body=%wide.region_2.5_spmd.sunk | while | flops 211122688 | bytes 11335781 | solution.py:122
  25.7 1.8 fusion.136
  29.8 1.8 fusion.136
  33.9 1.8 fusion.136
  38.0 1.8 fusion.136
  40.4 2.0 copy.68
  43.5 4.7 fusion.77
  50.1 223.8 %all-reduce.7.cloned.1.call-done = f32[2048,768]{1,0:T(8,128)} async-done(((f32[2048,768]{1,0:T(8,128)}), f32[2048,768]{1,0:T(8,128)}) %all-reduce.7.cloned.1.call-update) | async-done | bytes 6291472 | tf_op jit(solution)/shard_map/psum | solution.py:124
  273.9 4.6 fusion.76
  281.2 5.4 multiply_convert_fusion.1
  286.6 1.7 copy-done.30
  288.3 4.5 fusion.78
  293.5 221.3 %all-reduce.9.cloned.1.call-done = f32[2048,768]{1,0:T(8,128)} async-done(((f32[2048,768]{1,0:T(8,128)}), f32[2048,768]{1,0:T(8,128)}) %all-reduce.9.cloned.1.call-update) | async-done | bytes 6291472 | tf_op jit(solution)/shard_map/psum | solution.py:137
  514.8 5.7 fusion.75
  522.3 3.0 fusion.64
  525.4 4.3 fusion.74
  529.8 7.5 convert_reduce_fusion.1
  537.2 1.6 copy-done.29
  538.9 4.6 fusion.79
  543.7 424.1 %all-gather.3.cloned.1.call-done = f32[8192,768]{1,0:T(8,128)} async-done(((f32[2048,768]{1,0:T(8,128)}), f32[8192,768]{1,0:T(8,128)}) %all-gather.3.cloned.1.call-update) | async-done | bytes 25165840 | tf_op jit(solution)/shard_map/all_gather | solution.py:160
  967.7 12.6 reduce_sum.232
  980.4 8.1 multiply_reduce_fusion.1
  988.5 4.3 fusion.73
  992.8 2.6 copy-done.3
  999.5 29.7 %while.27 = (s32[]{:T(128)}, bf16[4,512,3,64]{1,3,2,0:T(8,128)(2,1)}, bf16[4,512,3,64]{1,3,2,0:T(8,128)(2,1)}, bf16[4,512,3,64]{1,3,2,0:T(8,128)(2,1)S(1)}, bf16...) while((s32[]{:T(128)}, ...), condition=%wide.region_19.20_spmd, body=%wide.region_17.19_spmd.sunk | while | flops 511146496 | bytes 26127484 | solution.py:175
  1000.4 1.5 fusion.145
  1007.9 1.5 fusion.145
  1029.2 2.0 copy.74
  1031.5 1.7 copy.73
  1036.3 3.7 add_add_fusion.2
  1040.4 7.1 fusion.82
  1047.5 7.2 fusion.70
  1054.7 1.7 convolution_bitcast_fusion
  1056.4 1.7 convolution_bitcast_fusion.2
  1058.0 1.7 convolution_bitcast_fusion.1
  1059.7 1.9 fusion.72
  1061.6 2.5 convert_reduce_fusion
  1064.6 196.8 %all-reduce.11.cloned.1.call-done = f32[2048,768]{1,0:T(8,128)} async-done(((f32[2048,768]{1,0:T(8,128)}), f32[2048,768]{1,0:T(8,128)}) %all-reduce.11.cloned.1.call-update) | async-done | bytes 6291472 | tf_op jit(solution)/shard_map/psum | solution.py:193
  1261.3 6.8 add_reduce_fusion
  1268.1 26.0 %all-reduce = (f32[192]{0:T(256)}, f32[192]{0:T(256)}, f32[768]{0:T(1024)}, f32[768]{0:T(1024)}, f32[768]{0:T(1024)}, /*index=5*/f32[768]{0:T(1024)}, f32[768]{0:T(1024)}, f32[768]{0:T(1024)}, f32[768]{0:T(1024)}) all-reduce(f32[192]{0:T(256)S(1)} %reduce_sum.236, f32[192]{0:T(256)S(1)} %reduce_sum.238, ...), channel_id=1, replica_groups=mesh['dp'=8,'mp'=4] {'dp'}, use_global_device_ids=true, to_apply=%region_23.24 | all-reduce | flops 5760 | bytes 46080 | tf_op jit(solution)/shard_map/psum | solution.py:194
  1294.2 85.5 %all-reduce.13.cloned.1.call-done = (f32[768,192]{0,1:T(8,128)}, f32[768,192]{0,1:T(8,128)}, f32[768,192]{0,1:T(8,128)}, f32[192,768]{1,0:T(8,128)}, f32[768,768]{1,0:T(8,128)}, /*index=5*/f32[768,768]{1,0:T(8,128)}) async-done(((f32[768,192]{0,1:T(8,128)}, f32[768,192]{0,1:T(8,128)}, f32[768,192]{0,1:T(8,128)}, f32[192,768]{1,0:T(8,128)}, f32[768,768]{1,0:T(8,128)}, /*index=5*/f32[768,768]{1,0:T(8,128)}), ...) | async-done | bytes 7077904 | tf_op jit(solution)/shard_map/psum | solution.py:194
  1379.6 2.1 copy.121
  1381.7 2.0 copy.122
  1383.7 1.9 copy.123
  1385.6 1.9 copy.124
  (183 shorter events, 62.6 us)
Async XLA Ops:
  7.2 274.0 %copy-start = (bf16[768,768]{1,0:T(8,128)(2,1)S(1)}, bf16[768,768]{1,0:T(8,128)(2,1)}, u32[]{:S(2)}) copy-start(bf16[768,768]{1,0:T(8,128)(2,1)} %param.33) | copy-start | bytes 3538948
  7.2 266.7 %all-reduce.7.cloned.1.call-start = ((), (), s32[]{:S(2)}) async-start(), calls=%async_computation | async-start | bytes 12582912 | tf_op jit(solution)/shard_map/psum | solution.py:124
  40.4 7.8 copy-start.12
  42.6 0.9 copy-start.7
  43.5 5.2 copy-start.22
  43.5 5.3 copy-start.23
  48.2 466.6 %all-reduce.9.cloned.1.call-start = ((), (), s32[]{:S(2)}) async-start(), calls=%async_computation.1 | async-start | bytes 12582912 | tf_op jit(solution)/shard_map/psum | solution.py:137
  278.5 2.7 copy-start.2
  281.2 5.4 copy-start.13
  281.2 7.1 copy-start.27
  286.6 1.7 copy-start.30
  292.8 0.7 copy-start.24
  292.8 0.7 copy-start.25
  292.8 0.7 copy-start.26
  292.8 674.9 %all-gather.3.cloned.1.call-start = ((), (), s32[]{:S(2)}) async-start(), calls=%async_computation.3 | async-start | bytes 31457280 | tf_op jit(solution)/shard_map/all_gather | solution.py:160
  520.5 1.9 copy-start.5
  522.3 7.4 slice-start.2
  525.4 4.4 copy-start.28
  525.4 4.3 slice-start.3
  529.7 7.5 copy-start.6
  537.2 1.6 copy-start.29
  543.4 717.9 %all-reduce.11.cloned.1.call-start = ((), (), s32[]{:S(2)}) async-start(), calls=%async_computation.2 | async-start | bytes 12582912 | tf_op jit(solution)/shard_map/psum | solution.py:193
  988.5 6.9 copy-start.16
  992.8 2.7 copy-start.3
  1029.2 4.8 copy-start.9
  1029.2 5.0 copy-start.17
  1034.0 1.3 copy-start.18
  1035.3 1.1 copy-start.19
  1040.1 339.5 %all-reduce.13.cloned.1.call-start = ((), (), s32[]{:S(2)}) async-start(), calls=%async_computation.4 | async-start | bytes 14155776 | tf_op jit(solution)/shard_map/psum | solution.py:194
  1040.4 7.1 copy-start.31
  1047.5 7.2 copy-start.4
  1054.7 5.0 slice-start
  1054.7 5.0 copy-start.8
  1056.4 3.3 slice-start.1
  1061.5 2.6 copy-start.10
  1061.6 2.6 copy-start.11
  1064.6 203.6 %copy-start.20 = (f32[768]{0:T(1024)S(1)}, f32[768]{0:T(1024)}, u32[]{:S(2)}) copy-start(f32[768]{0:T(1024)} %get-tuple-element.167) | copy-start | bytes 9220
  1064.6 203.6 %copy-start.21 = (f32[768]{0:T(1024)S(1)}, f32[768]{0:T(1024)}, u32[]{:S(2)}) copy-start(f32[768]{0:T(1024)} %get-tuple-element.238) | copy-start | bytes 9220
  1379.6 7.9 copy-start.15
  1379.6 9.3 copy-start.14
  1379.6 10.7 copy-start.1
Sparse Core Ops, SparseCore 0:
  48.3 225.5 all-reduce.6
  292.9 221.7 all-reduce.8
  543.6 424.1 all-gather.2
  1040.2 221.0 all-reduce.10
  1266.4 113.1 all-reduce.12
